TPU v7x, 32 devices: a whole 2x2x4 slice. The times are simulated.
32 devices in a mesh: ctx: 16 (over z, x, core), head: 2 (over y).
Axes of the slice: x: 2, y: 2, z: 4, core: 2. Of those that a mesh axis runs over, the one named last changes fastest.
Arguments:
- queries: bfloat16 [64, 2048], P(('ctx', 'head')), may hold values from -150 to 150
- new_block_keys: bfloat16 [64, 512], P(('ctx', 'head')), may hold values from -6 to 6
- new_block_values: bfloat16 [64, 512], P(('ctx', 'head')), may hold values from -6 to 6
- stored_keys: bfloat16 [7168, 512], P('ctx', 'head'), may hold values from -6 to 6
- stored_values: bfloat16 [7168, 512], P('ctx', 'head'), may hold values from -6 to 6
- stretch_start: int32 [1], replicated, may hold values from 3584 to 7168
- block_order: int32 [32], replicated, may hold values from 0 to 31, each once
Outputs:
- attended: bfloat16 [64, 2048], P(('ctx', 'head'))
Inputs may be any that keep to these rules, and one draw needn't show every extreme that they name: `block_order`: each value appears once.
All inputs are finite; a program needn't handle non-finite values.
Results may differ from a plain program's by a relative error of at most 0.0049.
Values may be sent and summed in bfloat16 or wider, within the bound.
A program may use at most 128 MiB of HBM per device.

v0:
```python
import math
import jax
import jax.numpy as jnp
from jax import lax
from jax.sharding import PartitionSpec as P

QUERY_HEADS = 16
KEY_VALUE_HEADS = 4
HEAD_WIDTH = 128
NEG_FILL = -1e30


def on_device(
    queries,
    new_block_keys,
    new_block_values,
    stored_keys,
    stored_values,
    stretch_start,
    block_order,
):
    local_query, local_keys, local_values = (
        lax.all_to_all(queries, "head", split_axis=1, concat_axis=0, tiled=True),
        lax.all_to_all(new_block_keys, "head", split_axis=1, concat_axis=0, tiled=True),
        lax.all_to_all(new_block_values, "head", split_axis=1, concat_axis=0, tiled=True),
    )
    query_rows = local_keys.shape[0]
    cache_rows = stored_keys.shape[0]
    kv_width = local_keys.shape[1]
    kv_heads = kv_width // HEAD_WIDTH
    query_group_width = QUERY_HEADS // KEY_VALUE_HEADS
    half_rows = query_rows // 2
    stretch_first = stretch_start[0]
    context = lax.axis_index("ctx")
    fresh_rows = context * query_rows + jnp.arange(query_rows, dtype=jnp.int32)
    fresh_pos = (
        stretch_first + block_order[fresh_rows // half_rows] * half_rows + fresh_rows % half_rows
    )
    cache_pos = context * cache_rows + jnp.arange(cache_rows, dtype=jnp.int32)
    key_pos = jnp.concatenate([fresh_pos, cache_pos])
    usable = jnp.concatenate([jnp.ones((query_rows,), dtype=bool), cache_pos < stretch_first])
    key_count = query_rows + cache_rows
    key_rows = jnp.concatenate([local_keys, stored_keys], axis=0).reshape(
        key_count, kv_heads, HEAD_WIDTH
    )
    value_rows = jnp.concatenate([local_values, stored_values], axis=0).reshape(
        key_count, kv_heads, HEAD_WIDTH
    )
    score_scale = 1.0 / math.sqrt(HEAD_WIDTH)
    piece = lax.all_gather(local_query, "ctx", axis=0, tiled=True)
    piece_rows = piece.shape[0]
    grouped = piece.reshape(piece_rows, kv_heads, query_group_width, HEAD_WIDTH)
    scores = (
        jnp.einsum("qhgd,khd->qhgk", grouped, key_rows, preferred_element_type=jnp.float32)
        * score_scale
    )
    row_index = jnp.arange(piece_rows, dtype=jnp.int32)
    query_pos = (
        stretch_first + block_order[row_index // half_rows] * half_rows + row_index % half_rows
    )
    allowed = usable[None, :] & (key_pos[None, :] <= query_pos[:, None])
    scores = jnp.where(allowed[:, None, None, :], scores, NEG_FILL)
    stretch_rows = scores.shape[0]
    peaks = lax.pmax(jnp.max(scores, axis=-1), "ctx")
    block_len = math.gcd(stretch_rows, 512)
    block_count = stretch_rows // block_len
    score_blocks = scores.reshape(block_count, block_len, kv_heads, query_group_width, key_count)
    peak_blocks = peaks.reshape(block_count, block_len, kv_heads, query_group_width)

    def weigh_block(inputs):
        block_scores, block_peaks = inputs
        weights = jnp.exp(block_scores - block_peaks[..., None])
        totals = jnp.sum(weights, axis=-1)
        product = jnp.einsum(
            "qhgk,khd->qhgd",
            weights.astype(jnp.bfloat16),
            value_rows,
            preferred_element_type=jnp.float32,
        )
        return (
            product.reshape(block_len, kv_heads * query_group_width * HEAD_WIDTH),
            totals.reshape(block_len, kv_heads * query_group_width),
        )

    sum_blocks, total_blocks = lax.map(weigh_block, (score_blocks, peak_blocks))
    weighted = sum_blocks.reshape(stretch_rows, kv_heads * query_group_width * HEAD_WIDTH)
    totals_all = total_blocks.reshape(stretch_rows, kv_heads * query_group_width)
    part_sums, part_totals = (
        lax.psum_scatter(weighted, "ctx", scatter_dimension=0, tiled=True),
        lax.psum_scatter(totals_all, "ctx", scatter_dimension=0, tiled=True),
    )
    own_rows = part_sums.shape[0]
    result = (
        part_sums.reshape(own_rows, kv_heads * query_group_width, HEAD_WIDTH)
        / part_totals[..., None]
    )
    result = result.reshape(own_rows, kv_heads * query_group_width * HEAD_WIDTH).astype(
        jnp.bfloat16
    )
    return lax.all_to_all(result, "head", split_axis=0, concat_axis=1, tiled=True)


def solution(mesh):
    return jax.shard_map(
        on_device,
        mesh=mesh,
        in_specs=(
            P(("ctx", "head"), None),
            P(("ctx", "head"), None),
            P(("ctx", "head"), None),
            P("ctx", "head"),
            P("ctx", "head"),
            P(),
            P(),
        ),
        out_specs=P(("ctx", "head"), None),
        check_vma=False,
    )
```

profile of v0, /device:TPU:0, one launch (start us, length us, event | category | flops | bytes accessed | tf_op | source)
XLA Modules:
  0.0 212.5 jit_solution(3873993751585935543)
XLA Ops:
  6.5 4.4 %all-to-all-start.1 = ((bf16[2,2,256]{2,0,1:T(2,128)(2,1)}), bf16[2,2,256]{2,0,1:T(2,128)(2,1)S(1)}, u32[]{:S(2)}, u32[]{:S(2)}) async-start(bf16[2,2,256]{2,0,1:T(2,128)(2,1)} %bitcast.60), calls=%async_computation.1 | async-start | bytes 4096 | tf_op jit(solution)/shard_map/all_to_all | solution.py:24
  11.6 0.6 copy-done.1
  12.3 0.6 gather_fusion
  12.9 0.8 gather_fusion.1
  13.7 0.9 copy-done.2
  14.7 3.3 %all-to-all-start = ((bf16[2,2,256]{2,0,1:T(2,128)(2,1)}), bf16[2,2,256]{2,0,1:T(2,128)(2,1)S(1)}, u32[]{:S(2)}, u32[]{:S(2)}) async-start(bf16[2,2,256]{2,0,1:T(2,128)(2,1)} %bitcast), calls=%async_computation | async-start | bytes 4096 | tf_op jit(solution)/shard_map/all_to_all | solution.py:25
  18.1 3.7 %all-to-all-done = bf16[2,2,256]{2,0,1:T(2,128)(2,1)S(1)} async-done(((bf16[2,2,256]{2,0,1:T(2,128)(2,1)}), bf16[2,2,256]{2,0,1:T(2,128)(2,1)S(1)}, u32[]{:S(2)}, u32[]{:S(2)}) %all-to-all-start) | async-done | bytes 2080 | tf_op jit(solution)/shard_map/all_to_all | solution.py:25
  21.8 3.2 %all-to-all-start.2 = ((bf16[2,2,1024]{2,0,1:T(2,128)(2,1)}), bf16[2,2,1024]{2,0,1:T(2,128)(2,1)S(1)}, u32[]{:S(2)}, u32[]{:S(2)}) async-start(bf16[2,2,1024]{2,0,1:T(2,128)(2,1)} %bitcast.11), calls=%async_computation.2 | async-start | bytes 16384 | tf_op jit(solution)/shard_map/all_to_all | solution.py:23
  25.1 0.1 compare_and_fusion
  25.2 0.6 copy-done.3
  25.9 0.6 dynamic-slice.2
  27.1 1.7 all-to-all-done.2
  28.9 22.4 %all-gather = bf16[16,4,1024]{2,1,0:T(4,128)(2,1)S(1)} all-gather(bf16[1,4,1024]{2,1,0:T(4,128)(2,1)S(1)} %reshape.221), channel_id=1, replica_groups=mesh['ctx'=16,'head'=2] {'ctx'}, dimensions={0}, use_global_device_ids=true | all-gather | bytes 139264 | tf_op jit(solution)/shard_map/all_gather | solution.py:50
  51.3 0.4 fusion.19
  51.7 29.8 %pmax.7 = f32[64,2,4]{0,2,1:T(4,128)S(1)} all-reduce(f32[64,2,4]{0,2,1:T(4,128)S(1)} %get-tuple-element.15), channel_id=1, replica_groups=mesh['ctx'=16,'head'=2] {'ctx'}, use_global_device_ids=true, to_apply=%region_1.2 | all-reduce | flops 512 | bytes 4096 | tf_op jit(solution)/shard_map/pmax | solution.py:64
  81.5 0.3 fusion.2
  81.9 29.5 %all-reduce.2 = f32[64,8]{0,1:T(8,128)S(1)} all-reduce(f32[64,8]{0,1:T(8,128)S(1)} %bitcast.57), channel_id=3, replica_groups=mesh['ctx'=16,'head'=2] {'ctx'}, use_global_device_ids=true, to_apply=%region_4.5.clone | all-reduce | flops 512 | bytes 4096
  111.5 0.4 convolution_bitcast_fusion
  111.9 0.2 copy.26
  112.1 0.8 reshape.203
  113.0 84.9 %all-reduce.5.cloned.1.call-done = f32[64,1024]{1,0:T(8,128)} async-done(((f32[64,1024]{1,0:T(8,128)}), f32[64,1024]{1,0:T(8,128)}) %all-reduce.5.cloned.1.call-update) | async-done | bytes 262160
  197.9 0.8 fusion.11
  198.7 6.4 %all_to_all.70 = bf16[2,2,1024]{2,1,0:T(2,128)(2,1)S(1)} all-to-all(bf16[2,2,1024]{2,1,0:T(2,128)(2,1)S(1)} %all_to_all.62), channel_id=1, replica_groups=mesh['ctx'=16,'head'=2] {'head'}, dimensions={0} | all-to-all | bytes 16384 | tf_op jit(solution)/shard_map/all_to_all | solution.py:100
  205.0 0.6 copy.47
  (30 shorter events, 0.7 us)
Async XLA Ops:
  6.5 7.1 %copy-start = (bf16[448,256]{1,0:T(8,128)(2,1)S(1)}, bf16[448,256]{1,0:T(8,128)(2,1)}, u32[]{:S(2)}) copy-start(bf16[448,256]{1,0:T(8,128)(2,1)} %param.10) | copy-start | bytes 688132
  6.5 8.2 %all-to-all-start.1 = ((bf16[2,2,256]{2,0,1:T(2,128)(2,1)}), bf16[2,2,256]{2,0,1:T(2,128)(2,1)S(1)}, u32[]{:S(2)}, u32[]{:S(2)}) async-start(bf16[2,2,256]{2,0,1:T(2,128)(2,1)} %bitcast.60), calls=%async_computation.1 | async-start | bytes 4096 | tf_op jit(solution)/shard_map/all_to_all | solution.py:24
  11.6 0.7 copy-start.1
  13.7 0.9 copy-start.2
  14.7 7.1 %all-to-all-start = ((bf16[2,2,256]{2,0,1:T(2,128)(2,1)}), bf16[2,2,256]{2,0,1:T(2,128)(2,1)S(1)}, u32[]{:S(2)}, u32[]{:S(2)}) async-start(bf16[2,2,256]{2,0,1:T(2,128)(2,1)} %bitcast), calls=%async_computation | async-start | bytes 4096 | tf_op jit(solution)/shard_map/all_to_all | solution.py:25
  21.8 7.0 %all-to-all-start.2 = ((bf16[2,2,1024]{2,0,1:T(2,128)(2,1)}), bf16[2,2,1024]{2,0,1:T(2,128)(2,1)S(1)}, u32[]{:S(2)}, u32[]{:S(2)}) async-start(bf16[2,2,1024]{2,0,1:T(2,128)(2,1)} %bitcast.11), calls=%async_computation.2 | async-start | bytes 16384 | tf_op jit(solution)/shard_map/all_to_all | solution.py:23
  25.1 172.8 %all-reduce.5.cloned.1.call-start = ((), (), s32[]{:S(2)}) async-start(), calls=%async_computation.4 | async-start | bytes 524288
  25.2 0.7 copy-start.3
Sparse Core Ops, SparseCore 0:
  113.0 84.7 all-reduce.4
where the time goes:
time: 213 us; the launch traced here: 212 us
  waiting for transfers between devices  90.3 us (42%)
  blocking collectives  88.1 us (41%)
  between operations  14.8 us (7%)
  starting transfers between devices  10.9 us (5%)
  local copies, waits for them, and re-layouts  6.24 us (3%)
    unnamed x2, waiting for transfers between devices  84.9 us
    pmax x1, blocking collectives, on_device(): peaks = lax.pmax(jnp.max(scores, axis=-1), 'ctx')  29.8 us
    unnamed x1, blocking collectives  29.5 us
    all_gather x1, blocking collectives, on_device(): piece = lax.all_gather(local_query, 'ctx', axis=0, tiled=True)  22.4 us
    all_to_all x1, blocking collectives, on_device(): lax.all_to_all(result, 'head', split_axis=0, concat_axis=1, tiled=True)  6.36 us
    all_to_all x1, starting transfers between devices, on_device(): lax.all_to_all(new_block_keys, 'head', split_axis=1, concat_axis=0, tiled...  4.37 us
  transfers between devices with their start and end apart: 4, of which 3 were waited for; matrix products, arithmetic and copies ran while one was open for 1% of the time, Pallas kernels for 0%

commit v1 on v0

--- a/solution.py
+++ b/solution.py
@@ -8,6 +8,23 @@
 KEY_VALUE_HEADS = 4
 HEAD_WIDTH = 128
 NEG_FILL = -1e30
+
+
+def laid_out(blocks, dim):
+    shape = list(blocks.shape[1:])
+    shape[dim] *= blocks.shape[0]
+    return jnp.moveaxis(blocks, 0, dim).reshape(shape)
+
+
+def grow_blocks(value, axis):
+    devices, index = (lax.axis_size(axis), lax.axis_index(axis))
+    parts, bit = (value[None], 1)
+    while bit < devices:
+        other = lax.ppermute(parts, axis, [(i, i ^ bit) for i in range(devices)])
+        low = index & bit == 0
+        parts = jnp.concatenate([jnp.where(low, parts, other), jnp.where(low, other, parts)])
+        bit *= 2
+    return parts
 
 
 def on_device(
@@ -47,7 +64,7 @@
         key_count, kv_heads, HEAD_WIDTH
     )
     score_scale = 1.0 / math.sqrt(HEAD_WIDTH)
-    piece = lax.all_gather(local_query, "ctx", axis=0, tiled=True)
+    piece = laid_out(grow_blocks(local_query, "ctx"), 0)
     piece_rows = piece.shape[0]
     grouped = piece.reshape(piece_rows, kv_heads, query_group_width, HEAD_WIDTH)
     scores = (

time: 213 us -> 199 us (0.934)
  blocking collectives: 88.1 us -> 65.3 us
  starting transfers between devices: 10.9 us -> 18.1 us
  waiting for transfers between devices: 90.3 us -> 92.8 us
    all_gather x1 -> x0, blocking collectives: 22.4 us -> none  [on_device(): piece = lax.all_gather(local_query, 'ctx', axis=0, tiled=True)]
    ppermute x0 -> x4, starting transfers between devices: none -> 7.21 us  [grow_blocks(): other = lax.ppermute(parts, axis, [(i, i ^ bit) for i in range(devices)])]
    ppermute x0 -> x4, waiting for transfers between devices: none -> 4.71 us  [grow_blocks(): other = lax.ppermute(parts, axis, [(i, i ^ bit) for i in range(devices)])]
  transfers between devices with their start and end apart: 4 -> 8, of which waited for: 3 -> 6; matrix products, arithmetic and copies ran while one was open for 1% -> 1% of each run, Pallas kernels for 0% -> 0%
where the time goes in v1:
time: 199 us; the launch traced here: 198 us
  waiting for transfers between devices  92.8 us (47%)
  blocking collectives  65.3 us (33%)
  starting transfers between devices  18.1 us (9%)
  between operations  14.9 us (7%)
  local copies, waits for them, and re-layouts  4.86 us (2%)
    unnamed x2, waiting for transfers between devices  84.9 us
    pmax x1, blocking collectives, on_device(): peaks = lax.pmax(jnp.max(scores, axis=-1), 'ctx')  29.5 us
    unnamed x1, blocking collectives  29.5 us
    ppermute x4, starting transfers between devices, grow_blocks(): other = lax.ppermute(parts, axis, [(i, i ^ bit) for i in range(devices)])  7.21 us
    all_to_all x1, blocking collectives, on_device(): lax.all_to_all(result, 'head', split_axis=0, concat_axis=1, tiled=True)  6.36 us
    ppermute x4, waiting for transfers between devices, grow_blocks(): other = lax.ppermute(parts, axis, [(i, i ^ bit) for i in range(devices)])  4.71 us
    all_to_all x1, starting transfers between devices, on_device(): lax.all_to_all(queries, 'head', split_axis=1, concat_axis=0, tiled=True)  4.37 us
  transfers between devices with their start and end apart: 8, of which 6 were waited for; matrix products, arithmetic and copies ran while one was open for 1% of the time, Pallas kernels for 0%

profile of v1, /device:TPU:0, one launch (start us, length us, event | category | flops | bytes accessed | tf_op | source)
XLA Modules:
  0.0 198.4 jit_solution(7553657963574069180)
XLA Ops:
  6.5 4.4 %all-to-all-start.2 = ((bf16[2,2,1024]{2,0,1:T(2,128)(2,1)}), bf16[2,2,1024]{2,0,1:T(2,128)(2,1)S(1)}, u32[]{:S(2)}, u32[]{:S(2)}) async-start(bf16[2,2,1024]{2,0,1:T(2,128)(2,1)} %bitcast.58), calls=%async_computation.2 | async-start | bytes 16384 | tf_op jit(solution)/shard_map/all_to_all | solution.py:40
  11.7 0.6 gather_fusion
  12.3 0.8 gather_fusion.1
  13.3 1.4 all-to-all-done.2
  14.7 3.2 %all-to-all-start.1 = ((bf16[2,2,256]{2,0,1:T(2,128)(2,1)}), bf16[2,2,256]{2,0,1:T(2,128)(2,1)S(1)}, u32[]{:S(2)}, u32[]{:S(2)}) async-start(bf16[2,2,256]{2,0,1:T(2,128)(2,1)} %bitcast.7), calls=%async_computation.1 | async-start | bytes 4096 | tf_op jit(solution)/shard_map/all_to_all | solution.py:41
  18.1 1.1 collective-permute-done
  19.2 2.0 %collective-permute-start.1 = (bf16[2,4,1024]{2,1,0:T(4,128)(2,1)S(1)}, bf16[2,4,1024]{2,1,0:T(4,128)(2,1)S(1)}, u32[]{:S(2)}, u32[]{:S(2)}) collective-permute-start(bf16[2,4,1024]{2,1,0:T(4,128)(2,1)S(1)} %pad_maximum_fusion.3), channel_id=1, source_target_pairs={{0,4},{2,6},{4,0},{6,2},{8,12},{10,14},{12,8},{14,10},{16,20},{18,... | collective-permute-start | bytes 49160 | tf_op jit(solution)/shard_map/ppermute | solution.py:23
  21.3 1.7 collective-permute-done.1
  23.1 2.1 %collective-permute-start.2 = (bf16[4,4,1024]{2,1,0:T(4,128)(2,1)S(1)}, bf16[4,4,1024]{2,1,0:T(4,128)(2,1)S(1)}, u32[]{:S(2)}, u32[]{:S(2)}) collective-permute-start(bf16[4,4,1024]{2,1,0:T(4,128)(2,1)S(1)} %pad_maximum_fusion.2), channel_id=1, source_target_pairs={{0,8},{2,10},{4,12},{6,14},{8,0},{10,2},{12,4},{14,6},{16,24},{18,... | collective-permute-start | bytes 98312 | tf_op jit(solution)/shard_map/ppermute | solution.py:23
  25.3 1.8 collective-permute-done.2
  27.2 3.1 %collective-permute-start.3 = (bf16[8,4,1024]{2,1,0:T(4,128)(2,1)S(1)}, bf16[8,4,1024]{2,1,0:T(4,128)(2,1)S(1)}, u32[]{:S(2)}, u32[]{:S(2)}) collective-permute-start(bf16[8,4,1024]{2,1,0:T(4,128)(2,1)S(1)} %pad_maximum_fusion.1), channel_id=1, source_target_pairs={{0,16},{2,18},{4,20},{6,22},{8,24},{10,26},{12,28},{14,30},{16,0},... | collective-permute-start | bytes 196616 | tf_op jit(solution)/shard_map/ppermute | solution.py:23
  30.3 3.2 %all-to-all-start = ((bf16[2,2,256]{2,0,1:T(2,128)(2,1)}), bf16[2,2,256]{2,0,1:T(2,128)(2,1)S(1)}, u32[]{:S(2)}, u32[]{:S(2)}) async-start(bf16[2,2,256]{2,0,1:T(2,128)(2,1)} %bitcast), calls=%async_computation | async-start | bytes 4096 | tf_op jit(solution)/shard_map/all_to_all | solution.py:42
  33.7 0.6 copy-done.3
  34.3 0.6 dynamic-slice.2
  35.6 1.7 all-to-all-done
  37.5 0.4 fusion.19
  37.9 29.5 %pmax.7 = f32[64,2,4]{0,2,1:T(4,128)S(1)} all-reduce(f32[64,2,4]{0,2,1:T(4,128)S(1)} %get-tuple-element.31), channel_id=1, replica_groups=mesh['ctx'=16,'head'=2] {'ctx'}, use_global_device_ids=true, to_apply=%region_1.2 | all-reduce | flops 512 | bytes 4096 | tf_op jit(solution)/shard_map/pmax | solution.py:81
  67.8 29.5 %all-reduce.2 = f32[64,8]{0,1:T(8,128)S(1)} all-reduce(f32[64,8]{0,1:T(8,128)S(1)} %bitcast.57), channel_id=3, replica_groups=mesh['ctx'=16,'head'=2] {'ctx'}, use_global_device_ids=true, to_apply=%region_4.5.clone | all-reduce | flops 512 | bytes 4096
  97.4 0.4 convolution_bitcast_fusion
  98.0 0.8 reshape.200
  98.9 84.9 %all-reduce.5.cloned.1.call-done = f32[64,1024]{1,0:T(8,128)} async-done(((f32[64,1024]{1,0:T(8,128)}), f32[64,1024]{1,0:T(8,128)}) %all-reduce.5.cloned.1.call-update) | async-done | bytes 262160
  183.8 0.8 fusion.11
  184.6 6.4 %all_to_all.67 = bf16[2,2,1024]{2,1,0:T(2,128)(2,1)S(1)} all-to-all(bf16[2,2,1024]{2,1,0:T(2,128)(2,1)S(1)} %all_to_all.59), channel_id=1, replica_groups=mesh['ctx'=16,'head'=2] {'head'}, dimensions={0} | all-to-all | bytes 16384 | tf_op jit(solution)/shard_map/all_to_all | solution.py:117
  190.9 0.6 copy.47
  (45 shorter events, 1.9 us)
Async XLA Ops:
  6.5 4.4 %copy-start = (bf16[448,256]{1,0:T(8,128)(2,1)S(1)}, bf16[448,256]{1,0:T(8,128)(2,1)}, u32[]{:S(2)}) copy-start(bf16[448,256]{1,0:T(8,128)(2,1)} %param.10) | copy-start | bytes 688132
  6.5 8.2 %all-to-all-start.2 = ((bf16[2,2,1024]{2,0,1:T(2,128)(2,1)}), bf16[2,2,1024]{2,0,1:T(2,128)(2,1)S(1)}, u32[]{:S(2)}, u32[]{:S(2)}) async-start(bf16[2,2,1024]{2,0,1:T(2,128)(2,1)} %bitcast.58), calls=%async_computation.2 | async-start | bytes 16384 | tf_op jit(solution)/shard_map/all_to_all | solution.py:40
  11.0 0.7 copy-start.1
  12.3 0.9 copy-start.2
  14.7 15.6 %all-to-all-start.1 = ((bf16[2,2,256]{2,0,1:T(2,128)(2,1)}), bf16[2,2,256]{2,0,1:T(2,128)(2,1)S(1)}, u32[]{:S(2)}, u32[]{:S(2)}) async-start(bf16[2,2,256]{2,0,1:T(2,128)(2,1)} %bitcast.7), calls=%async_computation.1 | async-start | bytes 4096 | tf_op jit(solution)/shard_map/all_to_all | solution.py:41
  18.0 1.2 collective-permute-start
  19.2 3.8 %collective-permute-start.1 = (bf16[2,4,1024]{2,1,0:T(4,128)(2,1)S(1)}, bf16[2,4,1024]{2,1,0:T(4,128)(2,1)S(1)}, u32[]{:S(2)}, u32[]{:S(2)}) collective-permute-start(bf16[2,4,1024]{2,1,0:T(4,128)(2,1)S(1)} %pad_maximum_fusion.3), channel_id=1, source_target_pairs={{0,4},{2,6},{4,0},{6,2},{8,12},{10,14},{12,8},{14,10},{16,20},{18,... | collective-permute-start | bytes 49160 | tf_op jit(solution)/shard_map/ppermute | solution.py:23
  23.1 4.0 %collective-permute-start.2 = (bf16[4,4,1024]{2,1,0:T(4,128)(2,1)S(1)}, bf16[4,4,1024]{2,1,0:T(4,128)(2,1)S(1)}, u32[]{:S(2)}, u32[]{:S(2)}) collective-permute-start(bf16[4,4,1024]{2,1,0:T(4,128)(2,1)S(1)} %pad_maximum_fusion.2), channel_id=1, source_target_pairs={{0,8},{2,10},{4,12},{6,14},{8,0},{10,2},{12,4},{14,6},{16,24},{18,... | collective-permute-start | bytes 98312 | tf_op jit(solution)/shard_map/ppermute | solution.py:23
  27.2 10.1 %collective-permute-start.3 = (bf16[8,4,1024]{2,1,0:T(4,128)(2,1)S(1)}, bf16[8,4,1024]{2,1,0:T(4,128)(2,1)S(1)}, u32[]{:S(2)}, u32[]{:S(2)}) collective-permute-start(bf16[8,4,1024]{2,1,0:T(4,128)(2,1)S(1)} %pad_maximum_fusion.1), channel_id=1, source_target_pairs={{0,16},{2,18},{4,20},{6,22},{8,24},{10,26},{12,28},{14,30},{16,0},... | collective-permute-start | bytes 196616 | tf_op jit(solution)/shard_map/ppermute | solution.py:23
  30.3 7.0 %all-to-all-start = ((bf16[2,2,256]{2,0,1:T(2,128)(2,1)}), bf16[2,2,256]{2,0,1:T(2,128)(2,1)S(1)}, u32[]{:S(2)}, u32[]{:S(2)}) async-start(bf16[2,2,256]{2,0,1:T(2,128)(2,1)} %bitcast), calls=%async_computation | async-start | bytes 4096 | tf_op jit(solution)/shard_map/all_to_all | solution.py:42
  33.5 150.3 %all-reduce.5.cloned.1.call-start = ((), (), s32[]{:S(2)}) async-start(), calls=%async_computation.4 | async-start | bytes 524288
  33.7 0.7 copy-start.3
Sparse Core Ops, SparseCore 0:
  98.9 84.8 all-reduce.4
